TPU v7x, 32 devices: a whole 2x2x4 slice. The times are simulated.
32 devices in a mesh: gx: 4 (over z), gy: 4 (over y, core), gz: 2 (over x).
Axes of the slice: x: 2, y: 2, z: 4, core: 2. Of those that a mesh axis runs over, the one named last changes fastest.
Arguments:
- node_irreps: bfloat16 [4, 4, 2, 16, 25, 128], P('gx', 'gy', 'gz'), may hold values from -5 to 11
- positions: float32 [4, 4, 2, 3, 16], P('gx', 'gy', 'gz'), may hold values from 0 to 6.8
- send_list: int32 [4, 4, 2, 8], P('gx', 'gy', 'gz'), may hold values from 0 to 15, as said below
- neighbours: int32 [4, 4, 2, 16, 32], P('gx', 'gy', 'gz'), may hold values from 0 to 231
- displacements: float32 [4, 4, 2, 3, 512], P('gx', 'gy', 'gz'), may hold values from -6 to 6
- order_zero: bfloat16 [640, 640], replicated, may hold values from -0.25 to 0.25
- order_one: bfloat16 [512, 1024], replicated, may hold values from -0.25 to 0.25
- order_two: bfloat16 [384, 768], replicated, may hold values from -0.3125 to 0.3125
- reciprocal_triples: int32 [1024, 3], replicated, may hold values from -6 to 6
- reciprocal_filter: float32 [1024, 128], replicated, may hold values from 0.1 to 1
- cotangent: float32 [4, 4, 2, 16, 128], P('gx', 'gy', 'gz'), may hold values from -5 to 11
Outputs:
- updated: bfloat16 [4, 4, 2, 16, 25, 128], P('gx', 'gy', 'gz')
- long_range: float32 [4, 4, 2, 16, 128], P('gx', 'gy', 'gz')
- charge_grad: float32 [4, 4, 2, 16, 128], P('gx', 'gy', 'gz')
- position_grad: float32 [4, 4, 2, 3, 16], P('gx', 'gy', 'gz')
Inputs may be any that keep to these rules, and one draw needn't show every extreme that they name: `send_list`: entries of one block are distinct atoms of that block.
All inputs are finite; a program needn't handle non-finite values.
Results may differ from a plain program's by a relative error of at most 0.0023.
Values may be sent and summed in bfloat16 or wider, within the bound.
No kernel may reach another device: no remote copies, remote signals or barrier semaphores. Data moves between devices by JAX's collectives and lax.ppermute only.
A program may use at most 64 MiB of HBM per device.

v0:
```python
import math
import jax
import jax.numpy as jnp
from jax import lax
from jax.sharding import PartitionSpec as P

highest = lax.Precision.HIGHEST
cell_length = 6.8
planar_floor = 0.25
radial_width = 64.0


def with_halo(block, sides, width):
    for axis, dim in sides:
        count = lax.axis_size(axis)
        forward = [(i, i + 1) for i in range(count - 1)]
        forward.append((count - 1, 0))
        backward = [(target, source) for source, target in forward]
        low = lax.ppermute(
            lax.slice_in_dim(block, block.shape[dim] - width, None, axis=dim), axis, forward
        )
        high = lax.ppermute(lax.slice_in_dim(block, 0, width, axis=dim), axis, backward)
        block = jnp.concatenate([low, block, high], axis=dim)
    return block


def harmonic_slot(degree, signed_order):
    return degree * degree + degree + signed_order


def kept_rows():
    layout = []
    for degree in range(5):
        for signed_order in range(-degree, degree + 1):
            layout.append(harmonic_slot(degree, signed_order))
    return layout


def edge_messages(
    lookup_table, displacement, neighbour_index, order_zero, order_one, order_two, layout
):
    atom_count = neighbour_index.shape[0]
    neighbour_count = neighbour_index.shape[1]
    flat_index = neighbour_index.reshape(-1)
    edge_count = flat_index.shape[0]
    feature_width = lookup_table.shape[2]
    source = lookup_table[flat_index]
    length_squared = jnp.sum(displacement * displacement, axis=0)
    radial = jnp.exp(-length_squared / radial_width) / math.sqrt(neighbour_count)
    planar = jnp.sqrt(
        displacement[0] * displacement[0] + displacement[1] * displacement[1] + planar_floor
    )
    cos_one = displacement[0] / planar
    sin_one = displacement[1] / planar

    def neighbour_sum(values):
        weighted = values * radial[:, None, None]
        return jnp.sum(
            weighted.reshape(atom_count, neighbour_count, values.shape[1], feature_width), axis=1
        )

    collected = {}
    zero_slots = [layout.index(harmonic_slot(degree, 0)) for degree in range(5)]
    zero_input = source[:, zero_slots, :].reshape(edge_count, 5 * feature_width)
    zero_output = jnp.dot(zero_input, order_zero, preferred_element_type=jnp.float32)
    summed_zero_part = neighbour_sum(zero_output.reshape(edge_count, 5, feature_width))
    for degree in range(5):
        collected[harmonic_slot(degree, 0)] = summed_zero_part[:, degree]
    rotations = (
        (1, cos_one, sin_one, order_one),
        (2, cos_one * cos_one - sin_one * sin_one, 2.0 * cos_one * sin_one, order_two),
    )
    for harmonic_order, cosine, sine_term, weight_pair in rotations:
        degrees = list(range(harmonic_order, 5))
        count_of_rows = len(degrees)
        plus_slots = [layout.index(harmonic_slot(degree, harmonic_order)) for degree in degrees]
        minus_slots = [layout.index(harmonic_slot(degree, -harmonic_order)) for degree in degrees]
        plus_part = source[:, plus_slots, :].astype(jnp.float32)
        minus_part = source[:, minus_slots, :].astype(jnp.float32)
        cosine_wide = cosine[:, None, None]
        sine_wide = sine_term[:, None, None]
        turned_plus = (cosine_wide * plus_part + sine_wide * minus_part).astype(jnp.bfloat16)
        turned_minus = (cosine_wide * minus_part - sine_wide * plus_part).astype(jnp.bfloat16)
        split_at = count_of_rows * feature_width
        stacked = jnp.concatenate(
            [turned_plus.reshape(edge_count, split_at), turned_minus.reshape(edge_count, split_at)],
            axis=0,
        )
        product = jnp.dot(stacked, weight_pair, preferred_element_type=jnp.float32)
        upper_half = product[:edge_count]
        lower_half = product[edge_count:]
        mixed_plus = (upper_half[:, :split_at] - lower_half[:, split_at:]).reshape(
            edge_count, count_of_rows, feature_width
        )
        mixed_minus = (upper_half[:, split_at:] + lower_half[:, :split_at]).reshape(
            edge_count, count_of_rows, feature_width
        )
        back_plus = neighbour_sum(cosine_wide * mixed_plus - sine_wide * mixed_minus)
        back_minus = neighbour_sum(sine_wide * mixed_plus + cosine_wide * mixed_minus)
        for position_in, degree in enumerate(degrees):
            collected[harmonic_slot(degree, harmonic_order)] = back_plus[:, position_in]
            collected[harmonic_slot(degree, -harmonic_order)] = back_minus[:, position_in]
    zero_block = jnp.zeros((atom_count, feature_width), jnp.float32)
    return jnp.stack([collected.get(slot_number, zero_block) for slot_number in range(25)], axis=1)


def table_product(table, values):
    return jnp.dot(table.T, values, precision=highest)


def local(
    node_irreps,
    positions,
    send_list,
    neighbours,
    displacements,
    order_zero,
    order_one,
    order_two,
    reciprocal_triples,
    reciprocal_filter,
    cotangent,
):
    local_irreps = node_irreps[0, 0, 0]
    atom_count = local_irreps.shape[0]
    size_x = lax.axis_size("gx")
    size_y = lax.axis_size("gy")
    size_z = lax.axis_size("gz")
    total_atom_count = atom_count * size_x * size_y * size_z
    scale_factor = 1.0 / math.sqrt(total_atom_count * reciprocal_filter.shape[0])
    corner = jnp.stack([lax.axis_index("gx"), lax.axis_index("gy"), lax.axis_index("gz")]).astype(
        jnp.float32
    )
    box = cell_length * jnp.array([size_x, size_y, size_z], jnp.float32)
    fractional = (positions[0, 0, 0] + cell_length * corner[:, None]) / box[:, None]
    wave_float = reciprocal_triples.astype(jnp.float32)
    phase = 2.0 * math.pi * jnp.dot(fractional.T, wave_float.T, precision=highest)
    cos_table = jnp.cos(phase)
    sin_table = jnp.sin(phase)
    charges = local_irreps[:, 0, :].astype(jnp.float32)
    grad_input = cotangent[0, 0, 0]
    raw_cos, raw_sin, charge_total, plane_cos, plane_sin = lax.psum(
        (
            table_product(cos_table, charges),
            table_product(sin_table, charges),
            jnp.sum(charges, axis=0),
            jnp.sum(cos_table, axis=0),
            jnp.sum(sin_table, axis=0),
        ),
        ("gx", "gy", "gz"),
    )
    resp_cos, resp_sin = lax.psum(
        (table_product(cos_table, grad_input), table_product(sin_table, grad_input)),
        ("gx", "gy", "gz"),
    )
    mean_charge = charge_total / total_atom_count
    centered = charges - mean_charge
    struct_cos = raw_cos - plane_cos[:, None] * mean_charge[None, :]
    struct_sin = raw_sin - plane_sin[:, None] * mean_charge[None, :]
    sent_rows = send_list[0, 0, 0]
    layout = kept_rows()
    arrived = with_halo(
        local_irreps[sent_rows][None, None, None], (("gx", 0), ("gy", 1), ("gz", 2)), 1
    )
    ghost_table = arrived.reshape((-1,) + local_irreps.shape[1:])
    lookup_table = jnp.concatenate([local_irreps, ghost_table], axis=0)
    messages = edge_messages(
        lookup_table,
        displacements[0, 0, 0],
        neighbours[0, 0, 0],
        order_zero,
        order_one,
        order_two,
        layout,
    )
    updated = (local_irreps.astype(jnp.float32) + messages).astype(jnp.bfloat16)
    long_range = scale_factor * (
        jnp.dot(cos_table, reciprocal_filter * struct_cos, precision=highest)
        + jnp.dot(sin_table, reciprocal_filter * struct_sin, precision=highest)
    )
    charge_term = scale_factor * (
        jnp.dot(cos_table, reciprocal_filter * resp_cos, precision=highest)
        + jnp.dot(sin_table, reciprocal_filter * resp_sin, precision=highest)
    )
    term_mean = (
        scale_factor
        * (
            jnp.dot(plane_cos, reciprocal_filter * resp_cos, precision=highest)
            + jnp.dot(plane_sin, reciprocal_filter * resp_sin, precision=highest)
        )
        / total_atom_count
    )
    charge_grad = charge_term - term_mean
    with_sin = jnp.dot(grad_input, (reciprocal_filter * struct_sin).T, precision=highest) + jnp.dot(
        centered, (reciprocal_filter * resp_sin).T, precision=highest
    )
    with_cos = jnp.dot(grad_input, (reciprocal_filter * struct_cos).T, precision=highest) + jnp.dot(
        centered, (reciprocal_filter * resp_cos).T, precision=highest
    )
    phase_grad = scale_factor * (cos_table * with_sin - sin_table * with_cos)
    position_grad = (2.0 * math.pi * jnp.dot(phase_grad, wave_float, precision=highest) / box).T
    return (
        updated[None, None, None],
        long_range[None, None, None],
        charge_grad[None, None, None],
        position_grad[None, None, None],
    )


def solution(mesh):
    return jax.shard_map(
        local,
        mesh=mesh,
        in_specs=(
            P("gx", "gy", "gz", None, None, None),
            P("gx", "gy", "gz", None, None),
            P("gx", "gy", "gz", None),
            P("gx", "gy", "gz", None, None),
            P("gx", "gy", "gz", None, None),
            P(),
            P(),
            P(),
            P(),
            P(),
            P("gx", "gy", "gz", None, None),
        ),
        out_specs=(
            P("gx", "gy", "gz", None, None, None),
            P("gx", "gy", "gz", None, None),
            P("gx", "gy", "gz", None, None),
            P("gx", "gy", "gz", None, None),
        ),
        check_vma=False,
    )
```

profile of v0, /device:TPU:0, one launch (start us, length us, event | category | flops | bytes accessed | tf_op | source)
XLA Modules:
  0.0 176.4 jit_solution(5121559690905927124)
XLA Ops:
  7.2 0.7 fusion.51
  8.0 0.9 copy.82
  9.5 5.1 %collective-permute-start.1 = (bf16[1,1,1,8,25,128]{5,4,3,2,1,0:T(8,128)(2,1)S(1)}, bf16[1,1,1,8,25,128]{5,4,3,2,1,0:T(8,128)(2,1)S(1)}, u32[]{:S(2)}, u32[]{:S(2)}) collective-permute-start(bf16[1,1,1,8,25,128]{5,4,3,2,1,0:T(8,128)(2,1)S(1)} %bitcast.173), channel_id=1, source_target_pairs={{8,0},{16,8},{24,16},{0,24},{9,1},{17,9},{25,17},{1,25},{10,2},{18... | collective-permute-start | bytes 153608 | tf_op jit(solution)/shard_map/ppermute | solution.py:22
  14.7 1.3 fusion.62
  16.1 1.4 fusion.40
  17.5 1.4 fusion.42
  18.9 2.5 %fusion.34 = f32[1024,128]{1,0:T(8,128)} fusion(f32[16,1024]{1,0:T(8,128)S(1)} %get-tuple-element.43, f32[1,1,1,16,128]{4,3,2,1,0:T(8,128)} %param.27), kind=kOutput, calls=%fused_computation.112 | convolution fusion | flops 25165824 | bytes 598016 | tf_op jit(solution)/shard_map/dot_general | solution.py:108
  21.4 1.8 %fusion.36 = f32[1024,128]{1,0:T(8,128)} fusion(f32[16,1024]{1,0:T(8,128)S(1)} %get-tuple-element.44, f32[1,1,1,16,128]{4,3,2,1,0:T(8,128)S(1)} %copy-done.11), kind=kOutput, calls=%fused_computation.114 | convolution fusion | flops 25165824 | bytes 598016 | tf_op jit(solution)/shard_map/dot_general | solution.py:108
  23.5 40.4 %all-reduce = (f32[128]{0:T(128)S(1)}, f32[1024]{0:T(1024)S(1)}, f32[1024]{0:T(1024)S(1)}) all-reduce(f32[128]{0:T(128)S(1)} %get-tuple-element.33, f32[1024]{0:T(1024)S(1)} %reduce_sum.87, f32[1024]{0:T(1024)S(1)} %reduce_sum.89), channel_id=1, replica_groups=mesh['gx'=4,'gy'=4,'gz'=2] {'gx','gy','gz'}, use_global_device_ids=true, to_apply=%region_10.0 | all-reduce | flops 2176 | bytes 17408 | tf_op jit(solution)/shard_map/psum | solution.py:142
  64.5 3.0 %collective-permute-done.3 = bf16[3,1,1,8,25,128]{5,4,3,2,1,0:T(8,128)(2,1)S(1)} collective-permute-done((bf16[3,1,1,8,25,128]{5,4,3,2,1,0:T(8,128)(2,1)S(1)}, bf16[3,1,1,8,25,128]{5,4,3,2,1,0:T(8,128)(2,1)S(1)}, u32[]{:S(2)}, u32[]{:S(2)}) %collective-permute-start.3) | collective-permute-done | bytes 153632 | tf_op jit(solution)/shard_map/ppermute | solution.py:22
  67.5 4.2 %collective-permute-done.2 = bf16[3,1,1,8,25,128]{5,4,3,2,1,0:T(8,128)(2,1)S(1)} collective-permute-done((bf16[3,1,1,8,25,128]{5,4,3,2,1,0:T(8,128)(2,1)S(1)}, bf16[3,1,1,8,25,128]{5,4,3,2,1,0:T(8,128)(2,1)S(1)}, u32[]{:S(2)}, u32[]{:S(2)}) %collective-permute-start.2) | collective-permute-done | bytes 153632 | tf_op jit(solution)/shard_map/ppermute | solution.py:19
  72.0 1.0 collective-permute-start.5
  73.0 1.1 collective-permute-start.4
  74.3 1.5 copy.58
  77.1 8.9 %collective-permute-done.5 = bf16[3,3,1,8,25,128]{5,3,4,2,1,0:T(8,128)(2,1)} collective-permute-done((bf16[3,3,1,8,25,128]{5,3,4,2,1,0:T(8,128)(2,1)S(1)}, bf16[3,3,1,8,25,128]{5,3,4,2,1,0:T(8,128)(2,1)}, u32[]{:S(2)}, u32[]{:S(2)}) %collective-permute-start.5) | collective-permute-done | bytes 460832 | tf_op jit(solution)/shard_map/ppermute | solution.py:22
  85.9 1.1 copy.53
  87.1 8.1 %collective-permute-done.4 = bf16[3,3,1,8,25,128]{5,3,4,2,1,0:T(8,128)(2,1)} collective-permute-done((bf16[3,3,1,8,25,128]{5,3,4,2,1,0:T(8,128)(2,1)S(1)}, bf16[3,3,1,8,25,128]{5,3,4,2,1,0:T(8,128)(2,1)}, u32[]{:S(2)}, u32[]{:S(2)}) %collective-permute-start.4) | collective-permute-done | bytes 460832 | tf_op jit(solution)/shard_map/ppermute | solution.py:19
  95.2 1.1 copy.52
  96.9 3.5 %gather_fusion.1 = bf16[512,25,128]{2,1,0:T(8,128)(2,1)} fusion(bf16[232,25,128]{2,1,0:T(8,128)(2,1)S(1)} %pad_maximum_fusion, s32[1024]{0:T(1024)S(1)} %get-tuple-element.75), kind=kCustom, calls=%fused_computation.1 | custom fusion | bytes 6555648 | tf_op jit(solution)/shard_map/gather | solution.py:47
  100.3 5.2 %copy.56 = bf16[512,25,128]{2,0,1:T(8,128)(2,1)} copy(bf16[512,25,128]{2,1,0:T(8,128)(2,1)} %gather_fusion.1) | data formatting | bytes 6553600 | tf_op jit(solution)/shard_map/gather | solution.py:47
  105.5 3.3 %gather_fusion.6 = bf16[3,512,128]{2,1,0:T(8,128)(2,1)} fusion(bf16[512,25,128]{2,0,1:T(8,128)(2,1)} %copy.56, s32[1024]{0:T(1024)S(1)} %get-tuple-element.70), kind=kCustom, calls=%fused_computation.6 | custom fusion | bytes 786444 | tf_op jit(solution)/shard_map/gather | solution.py:79
  108.8 2.5 %gather_fusion.5 = bf16[3,512,128]{2,1,0:T(8,128)(2,1)S(1)} fusion(bf16[512,25,128]{2,0,1:T(8,128)(2,1)} %copy.56, s32[1024]{0:T(1024)S(1)} %get-tuple-element.71), kind=kCustom, calls=%fused_computation.5 | custom fusion | bytes 786444 | tf_op jit(solution)/shard_map/gather | solution.py:78
  111.7 1.0 convert_bitcast_fusion.2
  112.7 1.2 copy.67
  113.9 3.4 %gather_fusion.4 = bf16[4,512,128]{2,1,0:T(8,128)(2,1)} fusion(bf16[512,25,128]{2,0,1:T(8,128)(2,1)} %copy.56, s32[1024]{0:T(1024)S(1)} %get-tuple-element.72), kind=kCustom, calls=%fused_computation.4 | custom fusion | bytes 1048592 | tf_op jit(solution)/shard_map/gather | solution.py:79
  117.3 3.4 %gather_fusion.3 = bf16[4,512,128]{2,1,0:T(8,128)(2,1)} fusion(bf16[512,25,128]{2,0,1:T(8,128)(2,1)} %copy.56, s32[1024]{0:T(1024)S(1)} %get-tuple-element.73), kind=kCustom, calls=%fused_computation.3 | custom fusion | bytes 1048592 | tf_op jit(solution)/shard_map/gather | solution.py:78
  120.7 2.6 %gather_fusion.2 = bf16[5,512,128]{2,1,0:T(8,128)(2,1)S(1)} fusion(bf16[512,25,128]{2,0,1:T(8,128)(2,1)} %copy.56, s32[1024]{0:T(1024)S(1)} %get-tuple-element.74), kind=kCustom, calls=%fused_computation.2 | custom fusion | bytes 1310740 | tf_op jit(solution)/shard_map/gather | solution.py:64
  123.3 1.1 copy.57
  124.4 2.2 %bitcast_reduce_fusion = f32[16,5,128]{2,0,1:T(8,128)S(1)} fusion(f32[512]{0:T(512)S(1)} %exponential_multiply_fusion, bf16[512,640,1]{0,1,2:T(8,128)(2,1)} %bitcast.182, bf16[5,128,640]{2,1,0:T(8,128)(2,1)} %bitcast.181), kind=kOutput, calls=%fused_computation.10 | convolution fusion | flops 420075520 | bytes 1517568 | tf_op jit(solution)/shard_map/dot_general | solution.py:65
  126.7 1.3 copy.61
  128.0 1.1 convert_bitcast_fusion
  129.1 1.3 copy.63
  130.5 1.4 fusion.26
  131.9 1.0 fusion.21
  132.9 1.0 slice_subtract_fusion.1
  134.3 1.5 reshape.294
  135.8 3.1 %multiply_reduce_fusion = (f32[16,3,128]{2,1,0:T(4,128)S(1)}, f32[16,3,128]{2,1,0:T(4,128)S(1)}) fusion(f32[16,32,3,128]{3,2,1,0:T(4,128)S(1)} %reshape.294, f32[16,32,3,128]{3,2,1,0:T(4,128)S(1)} %reshape.293, f32[16,32]{1,0:T(8,128)S(1)} %div.88, f32[16,32]{1,0:T(8,128)} %get-tuple-element.60, f32[16,32]{1,0:T(8,128)} %get-tuple-element.59), kind=kLoop, calls=%fused_computation.50 | loop fusion | flops 1953792 | bytes 1628160 | tf_op jit(solution)/shard_map/reduce_sum | solution.py:58
  139.3 1.3 fusion.13
  140.6 1.8 %slice_subtract_fusion = (f32[512,512]{1,0:T(8,128)}, f32[512,512]{1,0:T(8,128)}) fusion(f32[1024,1024]{1,0:T(8,128)S(1)} %fusion.13), kind=kLoop, calls=%fused_computation.35 | loop fusion | flops 524288 | bytes 6291456 | tf_op jit(solution)/shard_map/sub | solution.py:92
  142.4 1.6 reshape.291
  144.1 2.6 %reshape.292 = f32[16,32,4,128]{3,2,1,0:T(4,128)} reshape(f32[512,512]{1,0:T(8,128)} %get-tuple-element.36) | data formatting | bytes 2097152 | tf_op jit(solution)/shard_map/reshape | solution.py:95
  146.7 3.7 %multiply_reduce_fusion.2 = (f32[16,4,128]{2,1,0:T(4,128)S(1)}, f32[16,4,128]{2,1,0:T(4,128)S(1)}) fusion(f32[16,32,4,128]{3,2,1,0:T(4,128)} %reshape.292, f32[16,32,4,128]{3,2,1,0:T(4,128)S(1)} %reshape.291, f32[16,32]{1,0:T(8,128)S(1)} %div.88, f32[16,32]{1,0:T(8,128)S(1)} %copy-done.13, f32[16,32]{1,0:T(8,128)S(1)} %copy-done.14), kind=kLoop, calls=%fused_computation.52 | loop fusion | flops 2605056 | bytes 2168832 | tf_op jit(solution)/shard_map/reduce_sum | solution.py:58
  151.3 8.9 %all-reduce.4.cloned.1.call-done = (f32[1024,128]{1,0:T(8,128)}, f32[1024,128]{1,0:T(8,128)}, f32[1024,128]{1,0:T(8,128)}, f32[1024,128]{1,0:T(8,128)}) async-done(((f32[1024,128]{1,0:T(8,128)}, f32[1024,128]{1,0:T(8,128)}, f32[1024,128]{1,0:T(8,128)}, f32[1024,128]{1,0:T(8,128)}), (f32[1024,128]{1,0:T(8,128)}, f32[1024,128]{1,0:T(8,128)}, f32[1024,128]{1,0:T(8,128)}, ...) | async-done | bytes 2097168 | tf_op jit(solution)/shard_map/psum | solution.py:142
  160.3 1.6 fusion.29
  161.8 1.7 convolution_bitcast_fusion
  165.0 0.7 convolution_bitcast_fusion.1
  165.7 1.1 fusion.8
  168.5 1.0 fusion.6
  (127 shorter events, 8.8 us)
Async XLA Ops:
  7.2 132.1 %copy-start = (bf16[512,1024]{1,0:T(8,128)(2,1)S(1)}, bf16[512,1024]{1,0:T(8,128)(2,1)}, u32[]{:S(2)}) copy-start(bf16[512,1024]{1,0:T(8,128)(2,1)} %param.23) | copy-start | bytes 3145732
  7.2 14.2 %copy-start.11 = (f32[1,1,1,16,128]{4,3,2,1,0:T(8,128)S(1)}, f32[1,1,1,16,128]{4,3,2,1,0:T(8,128)}, u32[]{:S(2)}) copy-start(f32[1,1,1,16,128]{4,3,2,1,0:T(8,128)} %param.27) | copy-start | bytes 24580
  7.2 153.1 %all-reduce.4.cloned.1.call-start = ((), (), s32[]{:S(2)}) async-start(), calls=%async_computation | async-start | bytes 4194304 | tf_op jit(solution)/shard_map/psum | solution.py:142
  9.5 54.4 %collective-permute-start.1 = (bf16[1,1,1,8,25,128]{5,4,3,2,1,0:T(8,128)(2,1)S(1)}, bf16[1,1,1,8,25,128]{5,4,3,2,1,0:T(8,128)(2,1)S(1)}, u32[]{:S(2)}, u32[]{:S(2)}) collective-permute-start(bf16[1,1,1,8,25,128]{5,4,3,2,1,0:T(8,128)(2,1)S(1)} %bitcast.173), channel_id=1, source_target_pairs={{8,0},{16,8},{24,16},{0,24},{9,1},{17,9},{25,17},{1,25},{10,2},{18... | collective-permute-start | bytes 153608 | tf_op jit(solution)/shard_map/ppermute | solution.py:22
  14.6 49.3 %collective-permute-start = (bf16[1,1,1,8,25,128]{5,4,3,2,1,0:T(8,128)(2,1)S(1)}, bf16[1,1,1,8,25,128]{5,4,3,2,1,0:T(8,128)(2,1)S(1)}, u32[]{:S(2)}, u32[]{:S(2)}) collective-permute-start(bf16[1,1,1,8,25,128]{5,4,3,2,1,0:T(8,128)(2,1)S(1)} %bitcast.174), channel_id=1, source_target_pairs={{0,8},{8,16},{16,24},{24,0},{1,9},{9,17},{17,25},{25,1},{2,10},{10... | collective-permute-start | bytes 153608 | tf_op jit(solution)/shard_map/ppermute | solution.py:19
  17.5 5.8 %copy-start.15 = (f32[1,1,1,3,512]{4,2,3,1,0:T(1,128)S(1)}, f32[1,1,1,3,512]{4,2,3,1,0:T(1,128)}, u32[]{:S(2)}) copy-start(f32[1,1,1,3,512]{4,2,3,1,0:T(1,128)} %param.21) | copy-start | bytes 18436
  17.5 5.9 %copy-start.20 = (s32[1,1,1,16,32]{4,3,2,1,0:T(8,128)S(1)}, s32[1,1,1,16,32]{4,3,2,1,0:T(8,128)}, u32[]{:S(2)}) copy-start(s32[1,1,1,16,32]{4,3,2,1,0:T(8,128)} %param.20) | copy-start | bytes 6148
  18.9 45.6 %copy-start.26 = (s32[5]{0:T(128)S(1)}, s32[5]{0:T(128)}, u32[]{:S(2)}) copy-start(s32[5]{0:T(128)} %constant.102) | copy-start | bytes 64
  18.9 45.6 %copy-start.24 = (s32[4]{0:T(128)S(1)}, s32[4]{0:T(128)}, u32[]{:S(2)}) copy-start(s32[4]{0:T(128)} %constant.104) | copy-start | bytes 52
  18.9 45.7 %copy-start.25 = (s32[4]{0:T(128)S(1)}, s32[4]{0:T(128)}, u32[]{:S(2)}) copy-start(s32[4]{0:T(128)} %constant.103) | copy-start | bytes 52
  23.2 50.8 %copy-start.22 = (s32[3]{0:T(128)S(1)}, s32[3]{0:T(128)}, u32[]{:S(2)}) copy-start(s32[3]{0:T(128)} %constant.106) | copy-start | bytes 40
  23.3 50.8 %copy-start.23 = (s32[3]{0:T(128)S(1)}, s32[3]{0:T(128)}, u32[]{:S(2)}) copy-start(s32[3]{0:T(128)} %constant.105) | copy-start | bytes 40
  23.3 51.1 %copy-start.8 = (bf16[640,640]{1,0:T(8,128)(2,1)S(1)}, bf16[640,640]{1,0:T(8,128)(2,1)}, u32[]{:S(2)}) copy-start(bf16[640,640]{1,0:T(8,128)(2,1)} %param.22) | copy-start | bytes 2457604
  63.9 3.6 %collective-permute-start.3 = (bf16[3,1,1,8,25,128]{5,4,3,2,1,0:T(8,128)(2,1)S(1)}, bf16[3,1,1,8,25,128]{5,4,3,2,1,0:T(8,128)(2,1)S(1)}, u32[]{:S(2)}, u32[]{:S(2)}) collective-permute-start(bf16[3,1,1,8,25,128]{5,4,3,2,1,0:T(8,128)(2,1)S(1)} %pad_maximum_fusion.3), channel_id=1, source_target_pairs={{2,0},{4,2},{6,4},{0,6},{3,1},{5,3},{7,5},{1,7},{10,8},{12,10},{14... | collective-permute-start | bytes 460808 | tf_op jit(solution)/shard_map/ppermute | solution.py:22
  64.0 7.7 %collective-permute-start.2 = (bf16[3,1,1,8,25,128]{5,4,3,2,1,0:T(8,128)(2,1)S(1)}, bf16[3,1,1,8,25,128]{5,4,3,2,1,0:T(8,128)(2,1)S(1)}, u32[]{:S(2)}, u32[]{:S(2)}) collective-permute-start(bf16[3,1,1,8,25,128]{5,4,3,2,1,0:T(8,128)(2,1)S(1)} %pad_maximum_fusion.3), channel_id=1, source_target_pairs={{0,2},{2,4},{4,6},{6,0},{1,3},{3,5},{5,7},{7,1},{8,10},{10,12},{12... | collective-permute-start | bytes 460808 | tf_op jit(solution)/shard_map/ppermute | solution.py:19
  72.0 14.0 %collective-permute-start.5 = (bf16[3,3,1,8,25,128]{5,3,4,2,1,0:T(8,128)(2,1)S(1)}, bf16[3,3,1,8,25,128]{5,3,4,2,1,0:T(8,128)(2,1)}, u32[]{:S(2)}, u32[]{:S(2)}) collective-permute-start(bf16[3,3,1,8,25,128]{5,3,4,2,1,0:T(8,128)(2,1)S(1)} %copy.50), channel_id=1, source_target_pairs={{1,0},{0,1},{3,2},{2,3},{5,4},{4,5},{7,6},{6,7},{9,8},{8,9},{11,10... | collective-permute-start | bytes 1382408 | tf_op jit(solution)/shard_map/ppermute | solution.py:22
  73.0 22.2 %collective-permute-start.4 = (bf16[3,3,1,8,25,128]{5,3,4,2,1,0:T(8,128)(2,1)S(1)}, bf16[3,3,1,8,25,128]{5,3,4,2,1,0:T(8,128)(2,1)}, u32[]{:S(2)}, u32[]{:S(2)}) collective-permute-start(bf16[3,3,1,8,25,128]{5,3,4,2,1,0:T(8,128)(2,1)S(1)} %copy.50), channel_id=1, source_target_pairs={{0,1},{1,0},{2,3},{3,2},{4,5},{5,4},{6,7},{7,6},{8,9},{9,8},{10,11... | collective-permute-start | bytes 1382408 | tf_op jit(solution)/shard_map/ppermute | solution.py:19
  124.4 2.2 %copy-start.6 = (bf16[4,512,128]{2,1,0:T(8,128)(2,1)S(1)}, bf16[4,512,128]{2,1,0:T(8,128)(2,1)}, u32[]{:S(2)}) copy-start(bf16[4,512,128]{2,1,0:T(8,128)(2,1)} %gather_fusion.3) | copy-start | bytes 1572868
  128.0 2.5 %copy-start.18 = (f32[512]{0:T(512)S(1)}, f32[512]{0:T(512)}, u32[]{:S(2)}) copy-start(f32[512]{0:T(512)} %get-tuple-element.65) | copy-start | bytes 6148
  128.0 2.5 %copy-start.19 = (f32[512]{0:T(512)S(1)}, f32[512]{0:T(512)}, u32[]{:S(2)}) copy-start(f32[512]{0:T(512)} %get-tuple-element.68) | copy-start | bytes 6148
  130.5 1.4 copy-start.9
  135.7 3.2 %copy-start.4 = (f32[512,4,128]{0,2,1:T(8,128)S(1)}, f32[512,4,128]{0,2,1:T(8,128)}, u32[]{:S(2)}) copy-start(f32[512,4,128]{0,2,1:T(8,128)} %copy.61) | copy-start | bytes 3145732
  135.7 3.2 %copy-start.5 = (f32[512,4,128]{0,2,1:T(8,128)S(1)}, f32[512,4,128]{0,2,1:T(8,128)}, u32[]{:S(2)}) copy-start(f32[512,4,128]{0,2,1:T(8,128)} %copy.63) | copy-start | bytes 3145732
  135.8 3.2 %copy-start.16 = (f32[512]{0:T(512)S(1)}, f32[512]{0:T(512)}, u32[]{:S(2)}) copy-start(f32[512]{0:T(512)} %get-tuple-element.66) | copy-start | bytes 6148
  135.8 3.2 %copy-start.17 = (f32[512]{0:T(512)S(1)}, f32[512]{0:T(512)}, u32[]{:S(2)}) copy-start(f32[512]{0:T(512)} %get-tuple-element.67) | copy-start | bytes 6148
  142.4 4.2 %copy-start.13 = (f32[16,32]{1,0:T(8,128)S(1)}, f32[16,32]{1,0:T(8,128)}, u32[]{:S(2)}) copy-start(f32[16,32]{1,0:T(8,128)} %get-tuple-element.61) | copy-start | bytes 6148
  142.4 4.2 %copy-start.14 = (f32[16,32]{1,0:T(8,128)S(1)}, f32[16,32]{1,0:T(8,128)}, u32[]{:S(2)}) copy-start(f32[16,32]{1,0:T(8,128)} %get-tuple-element.62) | copy-start | bytes 6148
  144.0 6.6 %copy-start.10 = (bf16[1,1,1,16,25,128]{5,3,4,2,1,0:T(8,128)(2,1)S(1)}, bf16[1,1,1,16,25,128]{5,3,4,2,1,0:T(8,128)(2,1)}, u32[]{:S(2)}) copy-start(bf16[1,1,1,16,25,128]{5,3,4,2,1,0:T(8,128)(2,1)} %param.17) | copy-start | bytes 307204
  146.6 13.6 %copy-start.1 = (f32[1024,128]{1,0:T(8,128)S(1)}, f32[1024,128]{1,0:T(8,128)}, u32[]{:S(2)}) copy-start(f32[1024,128]{1,0:T(8,128)} %param.26) | copy-start | bytes 1572868
  160.2 3.3 %copy-start.3 = (f32[1024,128]{1,0:T(8,128)S(1)}, f32[1024,128]{1,0:T(8,128)}, u32[]{:S(2)}) copy-start(f32[1024,128]{1,0:T(8,128)} %get-tuple-element.31) | copy-start | bytes 1572868
  163.6 1.4 copy-start.7
  164.4 2.4 %copy-start.2 = (f32[1024,128]{1,0:T(8,128)S(1)}, f32[1024,128]{1,0:T(8,128)}, u32[]{:S(2)}) copy-start(f32[1024,128]{1,0:T(8,128)} %get-tuple-element.32) | copy-start | bytes 1572868
  165.0 2.4 %copy-start.12 = (s32[1024,3]{0,1:T(4,128)S(1)}, s32[1024,3]{0,1:T(4,128)}, u32[]{:S(2)}) copy-start(s32[1024,3]{0,1:T(4,128)} %param.25) | copy-start | bytes 36868
  165.0 2.4 %copy-start.21 = (f32[3]{0:T(128)S(1)}, f32[3]{0:T(128)}, u32[]{:S(2)}) copy-start(f32[3]{0:T(128)} %constant.100) | copy-start | bytes 40
Sparse Core Ops, SparseCore 0:
  23.4 136.8 all-reduce.3
where the time goes:
time: 177 us; the launch traced here: 176 us
  local copies, waits for them, and re-layouts  41.7 us (24%)
  blocking collectives  40.4 us (23%)
  waiting for transfers between devices  33.1 us (19%)
  matrix products  21.6 us (12%)
  other arithmetic  17.1 us (10%)
  between operations  14.7 us (8%)
  starting transfers between devices  7.82 us (4%)
    psum x1, blocking collectives, local(): lax.psum((table_product(cos_table, charges), table_product(sin_table, cha...  40.4 us
    ppermute x3, waiting for transfers between devices, with_halo(): lax.ppermute(lax.slice_in_dim(block, block.shape[dim] - width, None, axis...  12.3 us
    ppermute x3, waiting for transfers between devices, with_halo(): lax.ppermute(lax.slice_in_dim(block, 0, width, axis=dim), axis, backward)  11.8 us
    psum x1, waiting for transfers between devices, local(): lax.psum((table_product(cos_table, charges), table_product(sin_table, cha...  8.93 us
    gather x2, local copies, waits for them, and re-layouts, edge_messages(): source = lookup_table[flat_index]  8.67 us
    dot_general x4, matrix products, table_product(): return jnp.dot(table.T, values, precision=highest)  7.14 us
    reduce_sum x2, other arithmetic, neighbour_sum(): jnp.sum(weighted.reshape(atom_count, neighbour_count, values.shape[1], fe...  6.74 us
    gather x2, local copies, waits for them, and re-layouts, edge_messages(): minus_part = source[:, minus_slots, :].astype(jnp.float32)  6.71 us
  transfers between devices with their start and end apart: 7, of which 5 were waited for; matrix products, arithmetic and copies ran while one was open for 39% of the time, Pallas kernels for 0%

commit v1 on v0

--- a/solution.py
+++ b/solution.py
@@ -8,6 +8,11 @@
 cell_length = 6.8
 planar_floor = 0.25
 radial_width = 64.0
+
+
+def by_each_axis(value, inner_axis, outer_axis):
+    partial = lax.psum(value, inner_axis)
+    return lax.psum(partial, outer_axis)
 
 
 def with_halo(block, sides, width):
@@ -139,7 +144,7 @@
     sin_table = jnp.sin(phase)
     charges = local_irreps[:, 0, :].astype(jnp.float32)
     grad_input = cotangent[0, 0, 0]
-    raw_cos, raw_sin, charge_total, plane_cos, plane_sin = lax.psum(
+    raw_cos, raw_sin, charge_total, plane_cos, plane_sin = by_each_axis(
         (
             table_product(cos_table, charges),
             table_product(sin_table, charges),
@@ -147,7 +152,8 @@
             jnp.sum(cos_table, axis=0),
             jnp.sum(sin_table, axis=0),
         ),
-        ("gx", "gy", "gz"),
+        "gx",
+        ("gy", "gz"),
     )
     resp_cos, resp_sin = lax.psum(
         (table_product(cos_table, grad_input), table_product(sin_table, grad_input)),

time: 177 us -> 288 us (1.63)
  waiting for transfers between devices: 33.1 us -> 148 us
  blocking collectives: 40.4 us -> 26.8 us
  other arithmetic: 17.1 us -> 21.7 us
    psum x1 -> x3, waiting for transfers between devices: 8.93 us -> 144 us  [the longest x1 88.7 us: local(): lax.psum((table_product(cos_table, grad_input), table_product(sin_table,...]
    psum x1 -> x2, blocking collectives: 40.4 us -> 26.8 us  [the longest x1 14.2 us: by_each_axis(): return lax.psum(partial, outer_axis)]
    ppermute x3, waiting for transfers between devices: 12.3 us -> 0.98 us  [with_halo(): lax.ppermute(lax.slice_in_dim(block, block.shape[dim] - width, None, axis...]
    ppermute x3, waiting for transfers between devices: 11.8 us -> 3.32 us  [with_halo(): lax.ppermute(lax.slice_in_dim(block, 0, width, axis=dim), axis, backward)]
  transfers between devices with their start and end apart: 7 -> 9, of which waited for: 5 -> 4; matrix products, arithmetic and copies ran while one was open for 39% -> 28% of each run, Pallas kernels for 0% -> 0%
where the time goes in v1:
time: 288 us; the launch traced here: 287 us
  waiting for transfers between devices  148 us (51%)
  local copies, waits for them, and re-layouts  42.8 us (15%)
  blocking collectives  26.8 us (9%)
  matrix products  24.4 us (8%)
  other arithmetic  21.7 us (8%)
  between operations  14.5 us (5%)
  starting transfers between devices  8.58 us (3%)
    psum x1, waiting for transfers between devices, local(): lax.psum((table_product(cos_table, grad_input), table_product(sin_table,...  88.7 us
    psum x1, waiting for transfers between devices, by_each_axis(): return lax.psum(partial, outer_axis)  55.2 us
    psum x1, blocking collectives, by_each_axis(): return lax.psum(partial, outer_axis)  14.2 us
    psum x1, blocking collectives, by_each_axis(): partial = lax.psum(value, inner_axis)  12.6 us
    gather x2, local copies, waits for them, and re-layouts, edge_messages(): source = lookup_table[flat_index]  8.78 us
    dot_general x4, matrix products, table_product(): return jnp.dot(table.T, values, precision=highest)  7.84 us
    reduce_sum x2, other arithmetic, neighbour_sum(): jnp.sum(weighted.reshape(atom_count, neighbour_count, values.shape[1], fe...  7.18 us
    ppermute x3, starting transfers between devices, with_halo(): lax.ppermute(lax.slice_in_dim(block, 0, width, axis=dim), axis, backward)  7.02 us
  transfers between devices with their start and end apart: 9, of which 4 were waited for; matrix products, arithmetic and copies ran while one was open for 28% of the time, Pallas kernels for 0%

profile of v1, /device:TPU:0, one launch (start us, length us, event | category | flops | bytes accessed | tf_op | source)
XLA Modules:
  0.0 287.2 jit_solution(5980326981510226291)
XLA Ops:
  9.5 5.1 %collective-permute-start.1 = (bf16[1,1,1,8,25,128]{5,4,3,2,1,0:T(8,128)(2,1)S(1)}, bf16[1,1,1,8,25,128]{5,4,3,2,1,0:T(8,128)(2,1)S(1)}, u32[]{:S(2)}, u32[]{:S(2)}) collective-permute-start(bf16[1,1,1,8,25,128]{5,4,3,2,1,0:T(8,128)(2,1)S(1)} %bitcast.173), channel_id=1, source_target_pairs={{8,0},{16,8},{24,16},{0,24},{9,1},{17,9},{25,17},{1,25},{10,2},{18... | collective-permute-start | bytes 153608 | tf_op jit(solution)/shard_map/ppermute | solution.py:27
  14.7 1.3 fusion.62
  16.0 2.5 fusion.34
  18.5 2.5 fusion.36
  21.2 1.4 fusion.40
  22.6 1.4 fusion.42
  24.4 12.6 %all-reduce.3 = (f32[128]{0:T(128)S(1)}, f32[1024]{0:T(1024)S(1)}, f32[1024]{0:T(1024)S(1)}) all-reduce(f32[128]{0:T(128)S(1)} %get-tuple-element.38, f32[1024]{0:T(1024)S(1)} %reduce_sum.87, f32[1024]{0:T(1024)S(1)} %reduce_sum.89), channel_id=1, replica_groups=mesh['gx'=4,'gy'=4,'gz'=2] {'gx'}, use_global_device_ids=true, to_apply=%region_12.0 | all-reduce | flops 2176 | bytes 17408 | tf_op jit(solution)/shard_map/psum | solution.py:14
  37.0 14.2 %all-reduce.1 = (f32[128]{0:T(128)S(1)}, f32[1024]{0:T(1024)S(1)}, f32[1024]{0:T(1024)S(1)}) all-reduce(f32[128]{0:T(128)S(1)} %get-tuple-element.33, f32[1024]{0:T(1024)S(1)} %get-tuple-element.34, f32[1024]{0:T(1024)S(1)} %get-tuple-element.35), channel_id=1, replica_groups=mesh['gx'=4,'gy'=4,'gz'=2] {'gy','gz'}, use_global_device_ids=true, to_apply=%region_13.0 | all-reduce | flops 2176 | bytes 17408 | tf_op jit(solution)/shard_map/psum | solution.py:15
  53.7 1.2 collective-permute-start.3
  55.6 1.3 copy.58
  57.6 3.3 %collective-permute-done.3 = bf16[3,1,1,8,25,128]{5,4,3,2,1,0:T(8,128)(2,1)S(1)} collective-permute-done((bf16[3,1,1,8,25,128]{5,4,3,2,1,0:T(8,128)(2,1)S(1)}, bf16[3,1,1,8,25,128]{5,4,3,2,1,0:T(8,128)(2,1)S(1)}, u32[]{:S(2)}, u32[]{:S(2)}) %collective-permute-start.3) | collective-permute-done | bytes 153632 | tf_op jit(solution)/shard_map/ppermute | solution.py:27
  61.8 1.0 pad_maximum_fusion.2
  63.7 1.4 collective-permute-start.4
  65.2 88.7 %all-reduce.9.cloned.1.call-done = (f32[1024,128]{1,0:T(8,128)}, f32[1024,128]{1,0:T(8,128)}) async-done(((f32[1024,128]{1,0:T(8,128)}, f32[1024,128]{1,0:T(8,128)}), (f32[1024,128]{1,0:T(8,128)}, f32[1024,128]{1,0:T(8,128)})) %all-reduce.9.cloned.1.call-update) | async-done | bytes 1048592 | tf_op jit(solution)/shard_map/psum | solution.py:158
  153.9 1.5 convolution_bitcast_fusion.3
  155.4 1.4 fusion.12
  157.3 1.0 fusion.6
  158.3 1.1 copy.53
  159.6 1.2 pad_maximum_fusion.1
  161.0 3.6 %gather_fusion.1 = bf16[512,25,128]{2,1,0:T(8,128)(2,1)} fusion(bf16[232,25,128]{2,1,0:T(8,128)(2,1)S(1)} %pad_maximum_fusion, s32[1024]{0:T(1024)} %get-tuple-element.80), kind=kCustom, calls=%fused_computation.1 | custom fusion | bytes 6555648 | tf_op jit(solution)/shard_map/gather | solution.py:52
  164.6 5.2 %copy.56 = bf16[512,25,128]{2,0,1:T(8,128)(2,1)} copy(bf16[512,25,128]{2,1,0:T(8,128)(2,1)} %gather_fusion.1) | data formatting | bytes 6553600 | tf_op jit(solution)/shard_map/gather | solution.py:52
  169.8 3.4 %gather_fusion.6 = bf16[3,512,128]{2,1,0:T(8,128)(2,1)} fusion(bf16[512,25,128]{2,0,1:T(8,128)(2,1)} %copy.56, s32[1024]{0:T(1024)} %get-tuple-element.75), kind=kCustom, calls=%fused_computation.6 | custom fusion | bytes 786444 | tf_op jit(solution)/shard_map/gather | solution.py:84
  173.2 2.7 gather_fusion.5
  176.3 1.0 convert_bitcast_fusion.2
  177.3 1.1 copy.67
  178.5 3.5 %gather_fusion.4 = bf16[4,512,128]{2,1,0:T(8,128)(2,1)} fusion(bf16[512,25,128]{2,0,1:T(8,128)(2,1)} %copy.56, s32[1024]{0:T(1024)} %get-tuple-element.77), kind=kCustom, calls=%fused_computation.4 | custom fusion | bytes 1048592 | tf_op jit(solution)/shard_map/gather | solution.py:84
  181.9 3.4 %gather_fusion.3 = bf16[4,512,128]{2,1,0:T(8,128)(2,1)} fusion(bf16[512,25,128]{2,0,1:T(8,128)(2,1)} %copy.56, s32[1024]{0:T(1024)} %get-tuple-element.78), kind=kCustom, calls=%fused_computation.3 | custom fusion | bytes 1048592 | tf_op jit(solution)/shard_map/gather | solution.py:83
  185.4 2.8 gather_fusion.2
  188.2 1.1 copy.57
  189.3 2.2 bitcast_reduce_fusion
  192.2 1.3 copy.61
  193.5 1.1 convert_bitcast_fusion
  194.6 1.3 copy.63
  195.9 1.4 fusion.26
  197.3 1.0 fusion.21
  198.4 1.0 slice_subtract_fusion.1
  199.4 1.5 reshape.293
  200.9 1.3 reshape.294
  202.2 3.8 %multiply_reduce_fusion = (f32[16,3,128]{2,1,0:T(4,128)S(1)}, f32[16,3,128]{2,1,0:T(4,128)S(1)}) fusion(f32[16,32,3,128]{3,2,1,0:T(4,128)} %reshape.294, f32[16,32,3,128]{3,2,1,0:T(4,128)S(1)} %reshape.293, f32[16,32]{1,0:T(8,128)S(1)} %div.88, f32[16,32]{1,0:T(8,128)S(1)} %copy-done.25, f32[16,32]{1,0:T(8,128)S(1)} %copy-done.24), kind=kLoop, calls=%fused_computation.50 | loop fusion | flops 1953792 | bytes 1628160 | tf_op jit(solution)/shard_map/reduce_sum | solution.py:63
  206.4 1.3 fusion.13
  207.7 1.8 slice_subtract_fusion
  209.5 1.6 reshape.291
  211.2 2.6 reshape.292
  213.8 3.4 %multiply_reduce_fusion.2 = (f32[16,4,128]{2,1,0:T(4,128)S(1)}, f32[16,4,128]{2,1,0:T(4,128)S(1)}) fusion(f32[16,32,4,128]{3,2,1,0:T(4,128)} %reshape.292, f32[16,32,4,128]{3,2,1,0:T(4,128)S(1)} %reshape.291, f32[16,32]{1,0:T(8,128)S(1)} %div.88, f32[16,32]{1,0:T(8,128)S(1)} %copy-done.22, f32[16,32]{1,0:T(8,128)S(1)} %copy-done.23), kind=kLoop, calls=%fused_computation.52 | loop fusion | flops 2605056 | bytes 2168832 | tf_op jit(solution)/shard_map/reduce_sum | solution.py:63
  218.3 55.2 %all-reduce.11.cloned.1.call-done = (f32[1024,128]{1,0:T(8,128)}, f32[1024,128]{1,0:T(8,128)}) async-done(((f32[1024,128]{1,0:T(8,128)}, f32[1024,128]{1,0:T(8,128)}), (f32[1024,128]{1,0:T(8,128)}, f32[1024,128]{1,0:T(8,128)})) %all-reduce.11.cloned.1.call-update) | async-done | bytes 1048592 | tf_op jit(solution)/shard_map/psum | solution.py:15
  273.5 1.6 fusion.29
  275.1 1.8 convolution_bitcast_fusion
  277.6 1.1 fusion.8
  (162 shorter events, 14.0 us)
Async XLA Ops:
  7.2 199.2 %copy-start = (bf16[512,1024]{1,0:T(8,128)(2,1)S(1)}, bf16[512,1024]{1,0:T(8,128)(2,1)}, u32[]{:S(2)}) copy-start(bf16[512,1024]{1,0:T(8,128)(2,1)} %param.23) | copy-start | bytes 3145732
  7.2 146.7 %all-reduce.9.cloned.1.call-start = ((), (), s32[]{:S(2)}) async-start(), calls=%async_computation | async-start | bytes 2097152 | tf_op jit(solution)/shard_map/psum | solution.py:158
  8.9 15.1 %copy-start.12 = (bf16[1,1,1,16,25,128]{5,4,3,2,1,0:T(8,128)(2,1)}, bf16[1,1,1,16,25,128]{5,4,3,2,1,0:T(8,128)(2,1)S(1)}, u32[]{:S(2)}) copy-start(bf16[1,1,1,16,25,128]{5,4,3,2,1,0:T(8,128)(2,1)S(1)} %copy.82) | copy-start | bytes 307204
  9.5 44.1 %collective-permute-start.1 = (bf16[1,1,1,8,25,128]{5,4,3,2,1,0:T(8,128)(2,1)S(1)}, bf16[1,1,1,8,25,128]{5,4,3,2,1,0:T(8,128)(2,1)S(1)}, u32[]{:S(2)}, u32[]{:S(2)}) collective-permute-start(bf16[1,1,1,8,25,128]{5,4,3,2,1,0:T(8,128)(2,1)S(1)} %bitcast.173), channel_id=1, source_target_pairs={{8,0},{16,8},{24,16},{0,24},{9,1},{17,9},{25,17},{1,25},{10,2},{18... | collective-permute-start | bytes 153608 | tf_op jit(solution)/shard_map/ppermute | solution.py:27
  14.6 39.0 %collective-permute-start = (bf16[1,1,1,8,25,128]{5,4,3,2,1,0:T(8,128)(2,1)S(1)}, bf16[1,1,1,8,25,128]{5,4,3,2,1,0:T(8,128)(2,1)S(1)}, u32[]{:S(2)}, u32[]{:S(2)}) collective-permute-start(bf16[1,1,1,8,25,128]{5,4,3,2,1,0:T(8,128)(2,1)S(1)} %bitcast.174), channel_id=1, source_target_pairs={{0,8},{8,16},{16,24},{24,0},{1,9},{9,17},{17,25},{25,1},{2,10},{10... | collective-permute-start | bytes 153608 | tf_op jit(solution)/shard_map/ppermute | solution.py:24
  16.0 141.3 %copy-start.8 = (f32[16,1024]{1,0:T(8,128)}, f32[16,1024]{1,0:T(8,128)S(1)}, u32[]{:S(2)}) copy-start(f32[16,1024]{1,0:T(8,128)S(1)} %get-tuple-element.48) | copy-start | bytes 196612
  18.5 5.5 %copy-start.27 = (f32[1,1,1,3,512]{4,2,3,1,0:T(1,128)S(1)}, f32[1,1,1,3,512]{4,2,3,1,0:T(1,128)}, u32[]{:S(2)}) copy-start(f32[1,1,1,3,512]{4,2,3,1,0:T(1,128)} %param.21) | copy-start | bytes 18436
  18.5 5.6 %copy-start.32 = (s32[1,1,1,16,32]{4,3,2,1,0:T(8,128)S(1)}, s32[1,1,1,16,32]{4,3,2,1,0:T(8,128)}, u32[]{:S(2)}) copy-start(s32[1,1,1,16,32]{4,3,2,1,0:T(8,128)} %param.20) | copy-start | bytes 6148
  21.1 31.9 %copy-start.40 = (s32[5]{0:T(128)S(1)}, s32[5]{0:T(128)}, u32[]{:S(2)}) copy-start(s32[5]{0:T(128)} %constant.102) | copy-start | bytes 64
  21.1 33.8 %copy-start.38 = (s32[4]{0:T(128)S(1)}, s32[4]{0:T(128)}, u32[]{:S(2)}) copy-start(s32[4]{0:T(128)} %constant.104) | copy-start | bytes 52
  21.1 33.8 %copy-start.39 = (s32[4]{0:T(128)S(1)}, s32[4]{0:T(128)}, u32[]{:S(2)}) copy-start(s32[4]{0:T(128)} %constant.103) | copy-start | bytes 52
  21.1 34.5 %copy-start.14 = (bf16[640,640]{1,0:T(8,128)(2,1)S(1)}, bf16[640,640]{1,0:T(8,128)(2,1)}, u32[]{:S(2)}) copy-start(bf16[640,640]{1,0:T(8,128)(2,1)} %param.22) | copy-start | bytes 2457604
  21.1 196.4 %all-reduce.13.cloned.1.call-start = ((), (), s32[]{:S(2)}) async-start(), calls=%async_computation.2 | async-start | bytes 2097152 | tf_op jit(solution)/shard_map/psum | solution.py:14
  22.6 34.4 %copy-start.36 = (s32[3]{0:T(128)S(1)}, s32[3]{0:T(128)}, u32[]{:S(2)}) copy-start(s32[3]{0:T(128)} %constant.106) | copy-start | bytes 40
  22.6 34.4 %copy-start.37 = (s32[3]{0:T(128)S(1)}, s32[3]{0:T(128)}, u32[]{:S(2)}) copy-start(s32[3]{0:T(128)} %constant.105) | copy-start | bytes 40
  24.0 249.5 %all-reduce.11.cloned.1.call-start = ((), (), s32[]{:S(2)}) async-start(), calls=%async_computation.1 | async-start | bytes 2097152 | tf_op jit(solution)/shard_map/psum | solution.py:15
  24.3 38.8 %copy-start.33 = (f32[512]{0:T(512)}, f32[512]{0:T(512)S(1)}, u32[]{:S(2)}) copy-start(f32[512]{0:T(512)S(1)} %exponential_multiply_fusion) | copy-start | bytes 6148
  51.2 102.7 %copy-start.20 = (f32[1024]{0:T(1024)}, f32[1024]{0:T(1024)S(1)}, u32[]{:S(2)}) copy-start(f32[1024]{0:T(1024)S(1)} %get-tuple-element.29) | copy-start | bytes 12292
  53.7 7.2 %collective-permute-start.3 = (bf16[3,1,1,8,25,128]{5,4,3,2,1,0:T(8,128)(2,1)S(1)}, bf16[3,1,1,8,25,128]{5,4,3,2,1,0:T(8,128)(2,1)S(1)}, u32[]{:S(2)}, u32[]{:S(2)}) collective-permute-start(bf16[3,1,1,8,25,128]{5,4,3,2,1,0:T(8,128)(2,1)S(1)} %pad_maximum_fusion.3), channel_id=1, source_target_pairs={{2,0},{4,2},{6,4},{0,6},{3,1},{5,3},{7,5},{1,7},{10,8},{12,10},{14... | collective-permute-start | bytes 460808 | tf_op jit(solution)/shard_map/ppermute | solution.py:27
  54.9 7.0 %collective-permute-start.2 = (bf16[3,1,1,8,25,128]{5,4,3,2,1,0:T(8,128)(2,1)S(1)}, bf16[3,1,1,8,25,128]{5,4,3,2,1,0:T(8,128)(2,1)}, u32[]{:S(2)}, u32[]{:S(2)}) collective-permute-start(bf16[3,1,1,8,25,128]{5,4,3,2,1,0:T(8,128)(2,1)S(1)} %pad_maximum_fusion.3), channel_id=1, source_target_pairs={{0,2},{2,4},{4,6},{6,0},{1,3},{3,5},{5,7},{7,1},{8,10},{10,12},{12... | collective-permute-start | bytes 460808 | tf_op jit(solution)/shard_map/ppermute | solution.py:24
  55.6 98.3 %copy-start.1 = (f32[1024,128]{1,0:T(8,128)S(1)}, f32[1024,128]{1,0:T(8,128)}, u32[]{:S(2)}) copy-start(f32[1024,128]{1,0:T(8,128)} %param.26) | copy-start | bytes 1572868
  63.1 95.2 %collective-permute-start.5 = (bf16[3,3,1,8,25,128]{5,3,4,2,1,0:T(8,128)(2,1)S(1)}, bf16[3,3,1,8,25,128]{5,3,4,2,1,0:T(8,128)(2,1)}, u32[]{:S(2)}, u32[]{:S(2)}) collective-permute-start(bf16[3,3,1,8,25,128]{5,3,4,2,1,0:T(8,128)(2,1)S(1)} %copy.50), channel_id=1, source_target_pairs={{1,0},{0,1},{3,2},{2,3},{5,4},{4,5},{7,6},{6,7},{9,8},{8,9},{11,10... | collective-permute-start | bytes 1382408 | tf_op jit(solution)/shard_map/ppermute | solution.py:27
  63.7 95.7 %collective-permute-start.4 = (bf16[3,3,1,8,25,128]{5,3,4,2,1,0:T(8,128)(2,1)S(1)}, bf16[3,3,1,8,25,128]{5,3,4,2,1,0:T(8,128)(2,1)S(1)}, u32[]{:S(2)}, u32[]{:S(2)}) collective-permute-start(bf16[3,3,1,8,25,128]{5,3,4,2,1,0:T(8,128)(2,1)S(1)} %copy.50), channel_id=1, source_target_pairs={{0,1},{1,0},{2,3},{3,2},{4,5},{5,4},{6,7},{7,6},{8,9},{9,8},{10,11... | collective-permute-start | bytes 1382408 | tf_op jit(solution)/shard_map/ppermute | solution.py:24
  153.9 2.9 %copy-start.4 = (f32[1024,128]{1,0:T(8,128)S(1)}, f32[1024,128]{1,0:T(8,128)}, u32[]{:S(2)}) copy-start(f32[1024,128]{1,0:T(8,128)} %get-tuple-element.26) | copy-start | bytes 1572868
  153.9 3.4 %copy-start.2 = (f32[1024,128]{1,0:T(8,128)S(1)}, f32[1024,128]{1,0:T(8,128)}, u32[]{:S(2)}) copy-start(f32[1024,128]{1,0:T(8,128)} %get-tuple-element.27) | copy-start | bytes 1572868
  185.4 3.9 %copy-start.34 = (f32[512]{0:T(512)S(1)}, f32[512]{0:T(512)}, u32[]{:S(2)}) copy-start(f32[512]{0:T(512)} %copy-done.33) | copy-start | bytes 6148
  189.3 2.8 copy-start.10
  193.5 2.4 copy-start.30
  193.5 2.4 copy-start.31
  199.4 2.8 copy-start.24
  199.4 2.8 copy-start.25
  200.9 5.2 %copy-start.28 = (f32[512]{0:T(512)S(1)}, f32[512]{0:T(512)}, u32[]{:S(2)}) copy-start(f32[512]{0:T(512)} %get-tuple-element.71) | copy-start | bytes 6148
  200.9 5.2 %copy-start.29 = (f32[512]{0:T(512)S(1)}, f32[512]{0:T(512)}, u32[]{:S(2)}) copy-start(f32[512]{0:T(512)} %get-tuple-element.72) | copy-start | bytes 6148
  202.2 3.9 %copy-start.6 = (f32[512,4,128]{0,2,1:T(8,128)S(1)}, f32[512,4,128]{0,2,1:T(8,128)}, u32[]{:S(2)}) copy-start(f32[512,4,128]{0,2,1:T(8,128)} %copy.61) | copy-start | bytes 3145732
  202.2 3.9 %copy-start.7 = (f32[512,4,128]{0,2,1:T(8,128)S(1)}, f32[512,4,128]{0,2,1:T(8,128)}, u32[]{:S(2)}) copy-start(f32[512,4,128]{0,2,1:T(8,128)} %copy.63) | copy-start | bytes 3145732
  209.5 4.2 %copy-start.22 = (f32[16,32]{1,0:T(8,128)S(1)}, f32[16,32]{1,0:T(8,128)}, u32[]{:S(2)}) copy-start(f32[16,32]{1,0:T(8,128)} %get-tuple-element.66) | copy-start | bytes 6148
  209.5 4.2 %copy-start.23 = (f32[16,32]{1,0:T(8,128)S(1)}, f32[16,32]{1,0:T(8,128)}, u32[]{:S(2)}) copy-start(f32[16,32]{1,0:T(8,128)} %get-tuple-element.67) | copy-start | bytes 6148
  211.1 6.1 %copy-start.17 = (f32[1,1,1,16,25,128]{5,3,4,2,1,0:T(8,128)S(1)}, f32[1,1,1,16,25,128]{5,3,4,2,1,0:T(8,128)}, u32[]{:S(2)}) copy-start(f32[1,1,1,16,25,128]{5,3,4,2,1,0:T(8,128)} %constant_dynamic-update-slice_fusion.22) | copy-start | bytes 614404
  213.7 3.8 %copy-start.16 = (bf16[1,1,1,16,25,128]{5,3,4,2,1,0:T(8,128)(2,1)S(1)}, bf16[1,1,1,16,25,128]{5,3,4,2,1,0:T(8,128)(2,1)}, u32[]{:S(2)}) copy-start(bf16[1,1,1,16,25,128]{5,3,4,2,1,0:T(8,128)(2,1)} %param.17) | copy-start | bytes 307204
  213.7 59.8 %copy-start.21 = (f32[1024]{0:T(1024)S(1)}, f32[1024]{0:T(1024)}, u32[]{:S(2)}) copy-start(f32[1024]{0:T(1024)} %copy-done.20) | copy-start | bytes 12292
  213.8 59.7 %copy-start.26 = (f32[128]{0:T(128)S(1)}, f32[128]{0:T(128)}, u32[]{:S(2)}) copy-start(f32[128]{0:T(128)} %broadcast_multiply_fusion) | copy-start | bytes 1540
  217.2 57.9 %copy-start.18 = (f32[1,1,1,16,128]{4,3,2,1,0:T(8,128)S(1)}, f32[1,1,1,16,128]{4,3,2,1,0:T(8,128)}, u32[]{:S(2)}) copy-start(f32[1,1,1,16,128]{4,3,2,1,0:T(8,128)} %param.27) | copy-start | bytes 24580
  217.6 60.0 %copy-start.9 = (f32[16,1024]{1,0:T(8,128)S(1)}, f32[16,1024]{1,0:T(8,128)}, u32[]{:S(2)}) copy-start(f32[16,1024]{1,0:T(8,128)} %copy-done.8) | copy-start | bytes 196612
  273.5 3.4 %copy-start.11 = (f32[1024,128]{1,0:T(8,128)S(1)}, f32[1024,128]{1,0:T(8,128)}, u32[]{:S(2)}) copy-start(f32[1024,128]{1,0:T(8,128)} %get-tuple-element.32) | copy-start | bytes 1572868
  275.1 3.6 %copy-start.5 = (f32[1024,128]{1,0:T(8,128)S(1)}, f32[1024,128]{1,0:T(8,128)}, u32[]{:S(2)}) copy-start(f32[1024,128]{1,0:T(8,128)} %get-tuple-element.26) | copy-start | bytes 1572868
  276.9 2.4 copy-start.3
  277.6 2.3 copy-start.19
  277.6 2.3 copy-start.35
  (2 other events, 2.7 us)
Sparse Core Ops, SparseCore 0:
  21.2 132.6 all-reduce.8
  156.3 50.9 all-reduce.12
  217.7 55.7 all-reduce.10
